TPU v7x, 128 devices: a whole 4x4x4 slice. The times are simulated.
128 devices in a mesh: dp: 16 (over y, x), expert: 4 (over z), tensor: 2 (over core).
Axes of the slice: x: 4, y: 4, z: 4, core: 2. Of those that a mesh axis runs over, the one named last changes fastest.
Arguments:
- tokens: bfloat16 [8192, 2048], P(('dp', 'expert')), may hold values from -6 to 6
- expert_ids: int32 [8192, 2], P(('dp', 'expert')), may hold values from 0 to 3, all different within a row; in each aligned block of 128 rows (0 to 127, 128 to 255, ...) at most 96 rows name the same one
- gate_values: float32 [8192, 2], P(('dp', 'expert')), may hold values from 0.1 to 1
- tag_labels: int32 [8192], P(('dp', 'expert')), may hold values from 0 to 31
- w_gate: bfloat16 [4, 2048, 7168], P('expert', 'dp', 'tensor'), may hold values from -0.125 to 0.125
- w_up: bfloat16 [4, 2048, 7168], P('expert', 'dp', 'tensor'), may hold values from -0.125 to 0.125
- w_down: bfloat16 [4, 7168, 2048], P('expert', 'tensor', 'dp'), may hold values from -0.0625 to 0.0625
- adapter_in: bfloat16 [4, 16, 2048], P('expert'), may hold values from -0.125 to 0.125
- adapter_out: bfloat16 [4, 16, 7168], P('expert', None, 'tensor'), may hold values from -1.5 to 1.5
- tag_weight: bfloat16 [2048, 32], replicated, may hold values from -0.125 to 0.125
Outputs:
- layer_out: bfloat16 [8192, 2048], P(('dp', 'expert'), 'tensor')
- in_gradient: float32 [4, 16, 2048], P('expert')
- out_gradient: float32 [4, 16, 7168], P('expert', None, 'tensor')
Inputs may be any that keep to these rules, and one draw needn't show every extreme that they name: `expert_ids`: each row names 2 different experts; the rows of one index of dp and expert name each expert at most 96 times, a bound that some block reaches.
All inputs are finite; a program needn't handle non-finite values.
Results may differ from a plain program's by a relative error of at most 0.017.
Values may be sent and summed in bfloat16 or wider, within the bound.
A program may use at most 128 MiB of HBM per device.

v0:
```python
import jax
import jax.numpy as jnp
from jax import lax
from jax.sharding import PartitionSpec as P

adapter_scale = 2.0


def contract_last(left, right):
    return lax.dot_general(
        left, right, (((1,), (1,)), ((), ())), preferred_element_type=jnp.float32
    )


def contract_first(left, right):
    return lax.dot_general(
        left, right, (((0,), (0,)), ((), ())), preferred_element_type=jnp.float32
    )


def tag_gradient(logits, tag_labels):
    exp_logits = jnp.exp(logits)
    probability = exp_logits / jnp.sum(exp_logits, axis=1, keepdims=True)
    labels_hot = (
        tag_labels[:, None] == jnp.arange(logits.shape[1], dtype=jnp.int32)[None, :]
    ).astype(jnp.float32)
    return probability - labels_hot


def local(
    tokens,
    expert_ids,
    gate_values,
    tag_labels,
    w_gate,
    w_up,
    w_down,
    adapter_in,
    adapter_out,
    tag_weight,
):
    experts = lax.axis_size("expert")
    shards = lax.axis_size("tensor")
    tok_count = tokens.shape[0]
    model_width = tokens.shape[1]
    share_width = model_width // shards
    capacity = 3 * tok_count // experts
    slot_count = experts * capacity
    flat_ids = expert_ids.reshape(-1)
    onehot = (flat_ids[:, None] == jnp.arange(experts, dtype=jnp.int32)[None, :]).astype(jnp.int32)
    before = jnp.cumsum(onehot, axis=0) - onehot
    position = jnp.sum(before * onehot, axis=1)
    slot_index = (flat_ids * capacity + position).reshape(tok_count, expert_ids.shape[1])
    matches = jnp.arange(slot_count, dtype=jnp.int32)[:, None, None] == slot_index[None, :, :]
    dispatch = jnp.sum(matches.astype(jnp.float32), axis=2).astype(jnp.bfloat16)
    combine = jnp.sum(jnp.where(matches, gate_values[None, :, :], jnp.float32(0.0)), axis=2).T
    outgoing = jnp.dot(dispatch, tokens, preferred_element_type=jnp.float32).astype(jnp.bfloat16)
    arrived = lax.all_to_all(
        outgoing.reshape(experts, capacity, model_width),
        "expert",
        split_axis=0,
        concat_axis=0,
        tiled=True,
    ).reshape(slot_count, model_width)
    gate_acc = jnp.dot(
        arrived,
        lax.all_gather(w_gate, "dp", axis=1, tiled=True)[0],
        preferred_element_type=jnp.float32,
    )
    up_acc = jnp.dot(
        arrived,
        lax.all_gather(w_up, "dp", axis=1, tiled=True)[0],
        preferred_element_type=jnp.float32,
    )
    low_rank = contract_last(arrived, adapter_in[0]).astype(jnp.bfloat16)
    up_full = up_acc + adapter_scale * jnp.dot(
        low_rank, adapter_out[0], preferred_element_type=jnp.float32
    )
    activated = jax.nn.silu(gate_acc)
    hidden = (activated * up_full).astype(jnp.bfloat16)
    down_full = lax.all_gather(w_down, "dp", axis=2, tiled=True)[0]
    partial_value = jnp.dot(hidden, down_full, preferred_element_type=jnp.float32)
    column_start = lax.axis_index("tensor") * share_width
    summed = lax.psum(partial_value, "tensor").astype(jnp.bfloat16)
    returned = lax.all_to_all(
        summed.reshape(experts, capacity, model_width),
        "expert",
        split_axis=0,
        concat_axis=0,
        tiled=True,
    ).reshape(slot_count, model_width)
    mixed_rows = tokens.astype(jnp.float32) + jnp.dot(
        combine, returned.astype(jnp.float32), precision=lax.Precision.HIGHEST
    )
    layer_full = mixed_rows.astype(jnp.bfloat16)
    logits = jnp.dot(layer_full, tag_weight, preferred_element_type=jnp.float32)
    logit_grad = tag_gradient(logits, tag_labels)
    upstream = jnp.dot(
        logit_grad, tag_weight.astype(jnp.float32).T, precision=lax.Precision.HIGHEST
    )
    slot_out = jnp.dot(combine.T, upstream, precision=lax.Precision.HIGHEST).astype(jnp.bfloat16)
    slot_grad = lax.all_to_all(
        slot_out.reshape(experts, capacity, model_width),
        "expert",
        split_axis=0,
        concat_axis=0,
        tiled=True,
    ).reshape(slot_count, model_width)
    layer_out = lax.dynamic_slice_in_dim(layer_full, column_start, share_width, 1)
    hidden_grad = contract_last(slot_grad, down_full)
    up_grad = (hidden_grad * activated).astype(jnp.bfloat16)
    out_local = adapter_scale * contract_first(low_rank, up_grad)
    low_grad = adapter_scale * contract_last(up_grad, adapter_out[0])
    in_local = lax.dot_general(
        low_grad,
        arrived.astype(jnp.float32),
        (((0,), (0,)), ((), ())),
        precision=lax.Precision.HIGHEST,
    )
    in_total = lax.psum(in_local.astype(jnp.bfloat16), ("dp", "tensor")).astype(jnp.float32)
    out_total = lax.psum(out_local.astype(jnp.bfloat16), "dp").astype(jnp.float32)
    return (layer_out, in_total[None], out_total[None])


def solution(mesh):
    in_specs = (
        P(("dp", "expert"), None),
        P(("dp", "expert"), None),
        P(("dp", "expert"), None),
        P(("dp", "expert")),
        P("expert", "dp", "tensor"),
        P("expert", "dp", "tensor"),
        P("expert", "tensor", "dp"),
        P("expert", None, None),
        P("expert", None, "tensor"),
        P(),
    )
    out_specs = (
        P(("dp", "expert"), "tensor"),
        P("expert", None, None),
        P("expert", None, "tensor"),
    )
    return jax.shard_map(local, mesh=mesh, in_specs=in_specs, out_specs=out_specs, check_vma=False)
```

profile of v0, /device:TPU:0, one launch (start us, length us, event | category | flops | bytes accessed | tf_op | source)
XLA Modules:
  0.0 610.8 jit_solution(16985919612496595279)
XLA Ops:
  7.2 0.7 all-gather.6.cloned.1.call-update
  8.0 0.7 all-gather.4.cloned.1.call-update
  8.7 0.7 all-gather.8.cloned.1.call-update
  9.4 0.8 copy.31
  10.5 1.2 reduce-window.6
  12.4 0.7 multiply_add_fusion
  13.1 0.8 convert_reduce_fusion
  13.9 0.6 convolution_convert_fusion.1
  14.4 25.9 %all_to_all.15 = bf16[4,96,2048]{2,1,0:T(8,128)(2,1)S(1)} all-to-all(bf16[4,96,2048]{2,1,0:T(8,128)(2,1)S(1)} %bitcast.78), channel_id=1, replica_groups=mesh['dp'=16,'expert'=4,'tensor'=2] {'expert'}, dimensions={0} | all-to-all | bytes 3145728 | tf_op jit(solution)/shard_map/all_to_all | solution.py:58
  40.9 72.1 %all-gather.6.cloned.1.call-done = bf16[1,2048,3584]{2,1,0:T(8,128)(2,1)} async-done(((bf16[1,128,3584]{2,1,0:T(8,128)(2,1)}), bf16[1,2048,3584]{2,1,0:T(8,128)(2,1)}) %all-gather.6.cloned.1.call-update) | async-done | bytes 14680080 | tf_op jit(solution)/shard_map/all_gather | solution.py:72
  113.0 11.5 %fusion.4 = f32[384,3584]{1,0:T(8,128)} fusion(bf16[384,2048]{1,0:T(8,128)(2,1)S(1)} %bitcast.75, bf16[1,2048,3584]{2,1,0:T(8,128)(2,1)} %all-gather.6.cloned.1.call-done), kind=kOutput, calls=%fused_computation.4 | convolution fusion | flops 5637144576 | bytes 21757952 | tf_op jit(solution)/shard_map/dot_general | solution.py:70
  124.5 90.7 %all-gather.4.cloned.1.call-done = bf16[1,2048,3584]{2,1,0:T(8,128)(2,1)} async-done(((bf16[1,128,3584]{2,1,0:T(8,128)(2,1)}), bf16[1,2048,3584]{2,1,0:T(8,128)(2,1)}) %all-gather.4.cloned.1.call-update) | async-done | bytes 14680080 | tf_op jit(solution)/shard_map/all_gather | solution.py:67
  215.2 11.1 %divide_multiply_fusion = f32[384,3584]{1,0:T(8,128)} fusion(bf16[384,2048]{1,0:T(8,128)(2,1)S(1)} %bitcast.76, bf16[1,2048,3584]{2,1,0:T(8,128)(2,1)} %all-gather.4.cloned.1.call-done), kind=kOutput, calls=%fused_computation.14 | convolution fusion | flops 5642649600 | bytes 21757952 | tf_op jit(solution)/shard_map/dot_general | solution.py:65
  226.4 99.8 %all-gather.8.cloned.1.call-done = bf16[1,3584,2048]{2,1,0:T(8,128)(2,1)} async-done(((bf16[1,3584,128]{2,1,0:T(8,128)(2,1)}), bf16[1,3584,2048]{2,1,0:T(8,128)(2,1)}) %all-gather.8.cloned.1.call-update) | async-done | bytes 14680080 | tf_op jit(solution)/shard_map/all_gather | solution.py:81
  326.1 15.2 %fusion.2 = f32[384,2048]{1,0:T(8,128)} fusion(bf16[1,3584,2048]{2,1,0:T(8,128)(2,1)} %all-gather.8.cloned.1.call-done, f32[384,3584]{1,0:T(8,128)} %divide_multiply_fusion, f32[384,3584]{1,0:T(8,128)} %fusion.4, bf16[384,16]{0,1:T(8,128)(2,1)S(1)} %convolution_convert_fusion.3, bf16[1,16,3584]{2,1,0:T(8,128)(2,1)S(1)} %copy-done.4), kind=kOutput, calls=%fused_computation.2 | convolution fusion | flops 5686689792 | bytes 28962816 | tf_op jit(solution)/shard_map/dot_general | solution.py:82
  341.3 12.2 %all-reduce.7 = bf16[384,2048]{1,0:T(8,128)(2,1)S(1)} all-reduce(f32[384,2048]{1,0:T(8,128)} %fusion.2), channel_id=1, replica_groups=mesh['dp'=16,'expert'=4,'tensor'=2] {'tensor'}, use_global_device_ids=true, to_apply=%region_5.6 | all-reduce | flops 786432 | bytes 4718592 | tf_op jit(solution)/shard_map/psum | solution.py:84
  353.6 25.5 %all_to_all.16 = bf16[4,96,2048]{2,1,0:T(8,128)(2,1)S(1)} all-to-all(bf16[4,96,2048]{2,1,0:T(8,128)(2,1)S(1)} %bitcast.80), channel_id=1, replica_groups=mesh['dp'=16,'expert'=4,'tensor'=2] {'expert'}, dimensions={0} | all-to-all | bytes 3145728 | tf_op jit(solution)/shard_map/all_to_all | solution.py:85
  379.0 1.0 fusion.21
  380.4 0.6 fusion.28
  381.0 3.7 convolution_convert_fusion
  384.8 4.4 all-to-all-start.2
  389.2 20.4 %all-to-all-done.2 = bf16[4,96,2048]{2,1,0:T(8,128)(2,1)} async-done(((bf16[4,96,2048]{2,1,0:T(8,128)(2,1)}), bf16[4,96,2048]{2,1,0:T(8,128)(2,1)}, u32[]{:S(2)}, u32[]{:S(2)}) %all-to-all-start.2) | async-done | bytes 1572896 | tf_op jit(solution)/shard_map/all_to_all | solution.py:102
  409.6 10.4 %fusion.13 = bf16[384,3584]{1,0:T(8,128)(2,1)S(1)} fusion(f32[384,3584]{1,0:T(8,128)} %divide_multiply_fusion, bf16[384,2048]{1,0:T(8,128)(2,1)} %bitcast.12, bf16[1,3584,2048]{2,1,0:T(8,128)(2,1)} %all-gather.8.cloned.1.call-done), kind=kOutput, calls=%fused_computation.12 | convolution fusion | flops 5639897088 | bytes 24510464 | tf_op jit(solution)/shard_map/dot_general | solution.py:10
  420.0 0.8 convolution_multiply_fusion.2
  420.9 0.6 copy-done.2
  421.4 1.4 fusion.22
  422.9 1.1 fusion.20
  424.0 0.7 constant_dynamic-slice_fusion
  424.7 92.3 %all-reduce.4.cloned.1.call-done = bf16[1,16,2048]{2,1,0:T(8,128)(2,1)} async-done(((bf16[1,16,2048]{2,1,0:T(8,128)(2,1)}), bf16[1,16,2048]{2,1,0:T(8,128)(2,1)}) %all-reduce.4.cloned.1.call-update) | async-done | bytes 65552 | tf_op jit(solution)/shard_map/psum | solution.py:120
  517.0 1.5 broadcast_in_dim.33
  518.5 84.1 %all-reduce.6.cloned.1.call-done = bf16[1,16,3584]{2,1,0:T(8,128)(2,1)} async-done(((bf16[1,16,3584]{2,1,0:T(8,128)(2,1)}), bf16[1,16,3584]{2,1,0:T(8,128)(2,1)}) %all-reduce.6.cloned.1.call-update) | async-done | bytes 114704 | tf_op jit(solution)/shard_map/psum | solution.py:121
  602.7 1.6 broadcast_in_dim.35
  (34 shorter events, 2.0 us)
Async XLA Ops:
  7.2 372.9 %copy-start = (bf16[2048,32]{0,1:T(8,128)(2,1)S(1)}, bf16[2048,32]{0,1:T(8,128)(2,1)}, u32[]{:S(2)}) copy-start(bf16[2048,32]{0,1:T(8,128)(2,1)} %param.19) | copy-start | bytes 393220
  7.2 6.7 %copy-start.3 = (bf16[128,2048]{1,0:T(8,128)(2,1)S(1)}, bf16[128,2048]{1,0:T(8,128)(2,1)}, u32[]{:S(2)}) copy-start(bf16[128,2048]{1,0:T(8,128)(2,1)} %param.10) | copy-start | bytes 1572868
  7.2 105.8 %all-gather.6.cloned.1.call-start = ((), (), s32[]{:S(2)}) async-start(), calls=%async_computation.4 | async-start | bytes 15597568 | tf_op jit(solution)/shard_map/all_gather | solution.py:72
  7.9 207.3 %all-gather.4.cloned.1.call-start = ((), (), s32[]{:S(2)}) async-start(), calls=%async_computation.3 | async-start | bytes 15597568 | tf_op jit(solution)/shard_map/all_gather | solution.py:67
  8.7 317.4 %all-gather.8.cloned.1.call-start = ((), (), s32[]{:S(2)}) async-start(), calls=%async_computation.5 | async-start | bytes 15597568 | tf_op jit(solution)/shard_map/all_gather | solution.py:81
  9.4 31.0 %copy-start.5 = (bf16[1,16,2048]{2,1,0:T(8,128)(2,1)S(1)}, bf16[1,16,2048]{2,1,0:T(8,128)(2,1)}, u32[]{:S(2)}) copy-start(bf16[1,16,2048]{2,1,0:T(8,128)(2,1)} %param.17) | copy-start | bytes 196612
  40.4 174.9 %copy-start.1 = (bf16[4,96,2048]{2,1,0:T(8,128)(2,1)}, bf16[4,96,2048]{2,1,0:T(8,128)(2,1)S(1)}, u32[]{:S(2)}) copy-start(bf16[4,96,2048]{2,1,0:T(8,128)(2,1)S(1)} %all_to_all.15) | copy-start | bytes 4718596
  124.5 201.6 %copy-start.4 = (bf16[1,16,3584]{2,1,0:T(8,128)(2,1)S(1)}, bf16[1,16,3584]{2,1,0:T(8,128)(2,1)}, u32[]{:S(2)}) copy-start(bf16[1,16,3584]{2,1,0:T(8,128)(2,1)} %param.18) | copy-start | bytes 344068
  353.6 26.8 %copy-start.6 = (s32[128]{0:T(128)S(1)}, s32[128]{0:T(128)}, u32[]{:S(2)}) copy-start(s32[128]{0:T(128)} %param.13) | copy-start | bytes 1540
  384.8 24.8 %all-to-all-start.2 = ((bf16[4,96,2048]{2,1,0:T(8,128)(2,1)}), bf16[4,96,2048]{2,1,0:T(8,128)(2,1)}, u32[]{:S(2)}, u32[]{:S(2)}) async-start(bf16[4,96,2048]{2,1,0:T(8,128)(2,1)} %bitcast.11), calls=%async_computation.2 | async-start | bytes 3145728 | tf_op jit(solution)/shard_map/all_to_all | solution.py:102
  389.1 127.9 %all-reduce.4.cloned.1.call-start = ((), (), s32[]{:S(2)}) async-start(), calls=%async_computation.6 | async-start | bytes 131072 | tf_op jit(solution)/shard_map/psum | solution.py:120
  420.0 1.4 copy-start.2
  422.8 179.9 %all-reduce.6.cloned.1.call-start = ((), (), s32[]{:S(2)}) async-start(), calls=%async_computation.7 | async-start | bytes 229376 | tf_op jit(solution)/shard_map/psum | solution.py:121
Sparse Core Ops, SparseCore 0:
  10.1 102.8 all-gather.5
  115.2 100.0 all-gather.3
  217.4 108.6 all-gather.7
  422.9 94.0 all-reduce.3
  520.7 81.9 all-reduce.5
where the time goes:
time: 611 us
  waiting for transfers between devices  462 us (76%)
  blocking collectives  63.6 us (10%)
  matrix products  58.3 us (10%)
  between operations  13.9 us (2%)
    all_gather x1, waiting for transfers between devices, local(): down_full = lax.all_gather(w_down, 'dp', axis=2, tiled=True)[0]  99.8 us
    psum x1, waiting for transfers between devices, local(): lax.psum(in_local.astype(jnp.bfloat16), ('dp', 'tensor'))  92.3 us
    all_gather x1, waiting for transfers between devices, local(): lax.all_gather(w_gate, 'dp', axis=1, tiled=True)[0]  90.7 us
    psum x1, waiting for transfers between devices, local(): lax.psum(out_local.astype(jnp.bfloat16), 'dp').astype(jnp.float32)  84.1 us
    all_gather x1, waiting for transfers between devices, local(): lax.all_gather(w_up, 'dp', axis=1, tiled=True)[0]  72.1 us
    all_to_all x1, blocking collectives, local(): lax.all_to_all(outgoing.reshape(experts, capacity, model_width), 'expert'...  25.9 us
    all_to_all x1, blocking collectives, local(): lax.all_to_all(summed.reshape(experts, capacity, model_width), 'expert',...  25.5 us
    all_to_all x1, waiting for transfers between devices, local(): lax.all_to_all(slot_out.reshape(experts, capacity, model_width), 'expert'...  20.4 us
  transfers between devices with their start and end apart: 6, of which 6 were waited for; matrix products, arithmetic and copies ran while one was open for 5% of the time, Pallas kernels for 0%

commit v1 on v0

--- a/solution.py
+++ b/solution.py
@@ -69,7 +69,9 @@
     )
     up_acc = jnp.dot(
         arrived,
-        lax.all_gather(w_up, "dp", axis=1, tiled=True)[0],
+        jnp.concatenate(
+            lax.all_to_all(jnp.stack([w_up] * lax.axis_size("dp")), "dp", 0, 0), axis=1
+        )[0],
         preferred_element_type=jnp.float32,
     )
     low_rank = contract_last(arrived, adapter_in[0]).astype(jnp.bfloat16)

time: 611 us -> 685 us (1.12)
  waiting for transfers between devices: 462 us -> 520 us
  local copies, waits for them, and re-layouts: 2.94 us -> 10.6 us
    all_to_all x0 -> x1, waiting for transfers between devices: none -> 249 us  [local(): lax.all_to_all(jnp.stack([w_up] * lax.axis_size('dp')), 'dp', 0, 0)]
    all_gather x1, waiting for transfers between devices: 90.7 us -> 0.01 us  [local(): lax.all_gather(w_gate, 'dp', axis=1, tiled=True)[0]]
    all_gather x1 -> x0, waiting for transfers between devices: 72.1 us -> none  [local(): lax.all_gather(w_up, 'dp', axis=1, tiled=True)[0]]
    all_gather x1, waiting for transfers between devices: 99.8 us -> 72.2 us  [local(): down_full = lax.all_gather(w_down, 'dp', axis=2, tiled=True)[0]]
    all_to_all x0 -> x1, starting transfers between devices: none -> 7.21 us  [local(): lax.all_to_all(jnp.stack([w_up] * lax.axis_size('dp')), 'dp', 0, 0)]
  transfers between devices with their start and end apart: 6 -> 6, of which waited for: 6 -> 5; matrix products, arithmetic and copies ran while one was open for 5% -> 6% of each run, Pallas kernels for 0% -> 0%
where the time goes in v1:
time: 685 us; the launch traced here: 684 us
  waiting for transfers between devices  520 us (76%)
  blocking collectives  63.8 us (9%)
  matrix products  59.4 us (9%)
  between operations  13.9 us (2%)
  starting transfers between devices  10.9 us (2%)
  local copies, waits for them, and re-layouts  10.6 us (2%)
    all_to_all x1, waiting for transfers between devices, local(): lax.all_to_all(jnp.stack([w_up] * lax.axis_size('dp')), 'dp', 0, 0)  249 us
    psum x1, waiting for transfers between devices, local(): lax.psum(in_local.astype(jnp.bfloat16), ('dp', 'tensor'))  92.3 us
    psum x1, waiting for transfers between devices, local(): lax.psum(out_local.astype(jnp.bfloat16), 'dp').astype(jnp.float32)  84.2 us
    all_gather x1, waiting for transfers between devices, local(): down_full = lax.all_gather(w_down, 'dp', axis=2, tiled=True)[0]  72.2 us
    all_to_all x1, blocking collectives, local(): lax.all_to_all(outgoing.reshape(experts, capacity, model_width), 'expert'...  25.9 us
    all_to_all x1, blocking collectives, local(): lax.all_to_all(summed.reshape(experts, capacity, model_width), 'expert',...  25.5 us
    all_to_all x1, waiting for transfers between devices, local(): lax.all_to_all(slot_out.reshape(experts, capacity, model_width), 'expert'...  20.3 us
    dot_general x1, matrix products, local(): jnp.dot(hidden, down_full, preferred_element_type=jnp.float32)  15.2 us
  transfers between devices with their start and end apart: 6, of which 5 were waited for; matrix products, arithmetic and copies ran while one was open for 6% of the time, Pallas kernels for 0%

profile of v1, /device:TPU:0, one launch (start us, length us, event | category | flops | bytes accessed | tf_op | source)
XLA Modules:
  0.0 684.2 jit_solution(16133766996469841863)
XLA Ops:
  7.2 0.7 all-gather.3.cloned.1.call-update
  8.0 0.7 all-gather.5.cloned.1.call-update
  8.7 0.9 copy.31
  9.8 1.2 reduce-window.6
  11.7 0.7 multiply_add_fusion
  12.4 0.8 convert_reduce_fusion
  13.2 1.6 convolution_convert_fusion.1
  14.8 25.9 %all_to_all.20 = bf16[4,96,2048]{2,1,0:T(8,128)(2,1)S(1)} all-to-all(bf16[4,96,2048]{2,1,0:T(8,128)(2,1)S(1)} %bitcast.78), channel_id=1, replica_groups=mesh['dp'=16,'expert'=4,'tensor'=2] {'expert'}, dimensions={0} | all-to-all | bytes 3145728 | tf_op jit(solution)/shard_map/all_to_all | solution.py:58
  40.7 6.5 stack.2
  47.2 7.2 %all-to-all-start.1 = ((bf16[16,1,128,3584]{3,2,1,0:T(8,128)(2,1)}), bf16[16,1,128,3584]{3,2,1,0:T(8,128)(2,1)}, u32[]{:S(2)}, u32[]{:S(2)}) async-start(bf16[16,1,128,3584]{3,2,1,0:T(8,128)(2,1)} %stack.2), calls=%async_computation.1 | async-start | bytes 29360128 | tf_op jit(solution)/shard_map/all_to_all | solution.py:73
  55.0 249.1 %all-to-all-done.1 = bf16[16,1,128,3584]{3,2,1,0:T(8,128)(2,1)} async-done(((bf16[16,1,128,3584]{3,2,1,0:T(8,128)(2,1)}), bf16[16,1,128,3584]{3,2,1,0:T(8,128)(2,1)}, u32[]{:S(2)}, u32[]{:S(2)}) %all-to-all-start.1) | async-done | bytes 14680096 | tf_op jit(solution)/shard_map/all_to_all | solution.py:73
  304.1 11.5 %fusion.37 = f32[384,3584]{1,0:T(8,128)} fusion(bf16[384,2048]{1,0:T(8,128)(2,1)S(1)} %bitcast.75, bf16[2048,3584]{1,0:T(8,128)(2,1)} %bitcast.6), kind=kOutput, calls=%fused_computation.50 | convolution fusion | flops 5637144576 | bytes 21757952 | tf_op jit(solution)/shard_map/dot_general | solution.py:70
  315.6 11.2 %divide_multiply_fusion = f32[384,3584]{1,0:T(8,128)} fusion(bf16[384,2048]{1,0:T(8,128)(2,1)S(1)} %bitcast.76, bf16[1,2048,3584]{2,1,0:T(8,128)(2,1)} %all-gather.3.cloned.1.call-done), kind=kOutput, calls=%fused_computation.12 | convolution fusion | flops 5642649600 | bytes 21757952 | tf_op jit(solution)/shard_map/dot_general | solution.py:65
  326.8 72.2 %all-gather.5.cloned.1.call-done = bf16[1,3584,2048]{2,1,0:T(8,128)(2,1)} async-done(((bf16[1,3584,128]{2,1,0:T(8,128)(2,1)}), bf16[1,3584,2048]{2,1,0:T(8,128)(2,1)}) %all-gather.5.cloned.1.call-update) | async-done | bytes 14680080 | tf_op jit(solution)/shard_map/all_gather | solution.py:83
  399.0 15.2 %fusion.2 = f32[384,2048]{1,0:T(8,128)} fusion(bf16[1,3584,2048]{2,1,0:T(8,128)(2,1)} %all-gather.5.cloned.1.call-done, f32[384,3584]{1,0:T(8,128)} %divide_multiply_fusion, f32[384,3584]{1,0:T(8,128)} %fusion.37, bf16[384,16]{0,1:T(8,128)(2,1)S(1)} %convolution_convert_fusion.3, bf16[1,16,3584]{2,1,0:T(8,128)(2,1)S(1)} %copy-done.6), kind=kOutput, calls=%fused_computation.2 | convolution fusion | flops 5686689792 | bytes 28962816 | tf_op jit(solution)/shard_map/dot_general | solution.py:84
  414.1 12.4 %all-reduce.7 = bf16[384,2048]{1,0:T(8,128)(2,1)S(1)} all-reduce(f32[384,2048]{1,0:T(8,128)} %fusion.2), channel_id=1, replica_groups=mesh['dp'=16,'expert'=4,'tensor'=2] {'tensor'}, use_global_device_ids=true, to_apply=%region_5.6 | all-reduce | flops 786432 | bytes 4718592 | tf_op jit(solution)/shard_map/psum | solution.py:86
  426.5 25.5 %all_to_all.21 = bf16[4,96,2048]{2,1,0:T(8,128)(2,1)S(1)} all-to-all(bf16[4,96,2048]{2,1,0:T(8,128)(2,1)S(1)} %bitcast.80), channel_id=1, replica_groups=mesh['dp'=16,'expert'=4,'tensor'=2] {'expert'}, dimensions={0} | all-to-all | bytes 3145728 | tf_op jit(solution)/shard_map/all_to_all | solution.py:87
  452.0 1.0 fusion.19
  453.4 0.6 fusion.26
  454.0 3.8 convolution_convert_fusion
  457.8 3.6 all-to-all-start.3
  461.4 20.3 %all-to-all-done.3 = bf16[4,96,2048]{2,1,0:T(8,128)(2,1)S(1)} async-done(((bf16[4,96,2048]{2,1,0:T(8,128)(2,1)}), bf16[4,96,2048]{2,1,0:T(8,128)(2,1)S(1)}, u32[]{:S(2)}, u32[]{:S(2)}) %all-to-all-start.3) | async-done | bytes 1572896 | tf_op jit(solution)/shard_map/all_to_all | solution.py:104
  481.7 1.2 copy-done.4
  482.9 10.4 %fusion.11 = bf16[384,3584]{1,0:T(8,128)(2,1)S(1)} fusion(f32[384,3584]{1,0:T(8,128)} %divide_multiply_fusion, bf16[384,2048]{1,0:T(8,128)(2,1)} %bitcast.81, bf16[1,3584,2048]{2,1,0:T(8,128)(2,1)} %all-gather.5.cloned.1.call-done), kind=kOutput, calls=%fused_computation.10 | convolution fusion | flops 5639897088 | bytes 24510464 | tf_op jit(solution)/shard_map/dot_general | solution.py:10
  493.3 0.8 convolution_multiply_fusion.2
  494.7 1.4 fusion.20
  496.1 1.1 fusion.18
  497.3 0.7 constant_dynamic-slice_fusion
  498.0 92.3 %all-reduce.4.cloned.1.call-done = bf16[1,16,2048]{2,1,0:T(8,128)(2,1)} async-done(((bf16[1,16,2048]{2,1,0:T(8,128)(2,1)}), bf16[1,16,2048]{2,1,0:T(8,128)(2,1)}) %all-reduce.4.cloned.1.call-update) | async-done | bytes 65552 | tf_op jit(solution)/shard_map/psum | solution.py:122
  590.3 1.5 broadcast_in_dim.33
  591.9 84.2 %all-reduce.6.cloned.1.call-done = bf16[1,16,3584]{2,1,0:T(8,128)(2,1)} async-done(((bf16[1,16,3584]{2,1,0:T(8,128)(2,1)}), bf16[1,16,3584]{2,1,0:T(8,128)(2,1)}) %all-reduce.6.cloned.1.call-update) | async-done | bytes 114704 | tf_op jit(solution)/shard_map/psum | solution.py:123
  676.0 1.6 broadcast_in_dim.35
  (38 shorter events, 2.5 us)
Async XLA Ops:
  7.2 445.9 %copy-start = (bf16[2048,32]{0,1:T(8,128)(2,1)S(1)}, bf16[2048,32]{0,1:T(8,128)(2,1)}, u32[]{:S(2)}) copy-start(bf16[2048,32]{0,1:T(8,128)(2,1)} %param.19) | copy-start | bytes 393220
  7.2 308.4 %all-gather.3.cloned.1.call-start = ((), (), s32[]{:S(2)}) async-start(), calls=%async_computation.4 | async-start | bytes 15597568 | tf_op jit(solution)/shard_map/all_gather | solution.py:67
  7.9 391.0 %all-gather.5.cloned.1.call-start = ((), (), s32[]{:S(2)}) async-start(), calls=%async_computation.5 | async-start | bytes 15597568 | tf_op jit(solution)/shard_map/all_gather | solution.py:83
  8.7 32.0 %copy-start.5 = (bf16[1,128,3584]{2,1,0:T(8,128)(2,1)S(1)}, bf16[1,128,3584]{2,1,0:T(8,128)(2,1)}, u32[]{:S(2)}) copy-start(bf16[1,128,3584]{2,1,0:T(8,128)(2,1)} %param.15) | copy-start | bytes 2752516
  40.7 274.9 %copy-start.1 = (bf16[4,96,2048]{2,1,0:T(8,128)(2,1)}, bf16[4,96,2048]{2,1,0:T(8,128)(2,1)S(1)}, u32[]{:S(2)}) copy-start(bf16[4,96,2048]{2,1,0:T(8,128)(2,1)S(1)} %all_to_all.20) | copy-start | bytes 4718596
  47.2 7.2 %copy-start.7 = (bf16[1,16,2048]{2,1,0:T(8,128)(2,1)S(1)}, bf16[1,16,2048]{2,1,0:T(8,128)(2,1)}, u32[]{:S(2)}) copy-start(bf16[1,16,2048]{2,1,0:T(8,128)(2,1)} %param.17) | copy-start | bytes 196612
  47.2 256.9 %all-to-all-start.1 = ((bf16[16,1,128,3584]{3,2,1,0:T(8,128)(2,1)}), bf16[16,1,128,3584]{3,2,1,0:T(8,128)(2,1)}, u32[]{:S(2)}, u32[]{:S(2)}) async-start(bf16[16,1,128,3584]{3,2,1,0:T(8,128)(2,1)} %stack.2), calls=%async_computation.1 | async-start | bytes 29360128 | tf_op jit(solution)/shard_map/all_to_all | solution.py:73
  315.6 83.4 %copy-start.6 = (bf16[1,16,3584]{2,1,0:T(8,128)(2,1)S(1)}, bf16[1,16,3584]{2,1,0:T(8,128)(2,1)}, u32[]{:S(2)}) copy-start(bf16[1,16,3584]{2,1,0:T(8,128)(2,1)} %param.18) | copy-start | bytes 344068
  414.1 37.9 %copy-start.3 = (bf16[128,2048]{1,0:T(8,128)(2,1)S(1)}, bf16[128,2048]{1,0:T(8,128)(2,1)}, u32[]{:S(2)}) copy-start(bf16[128,2048]{1,0:T(8,128)(2,1)} %param.10) | copy-start | bytes 1572868
  426.5 26.8 %copy-start.8 = (s32[128]{0:T(128)S(1)}, s32[128]{0:T(128)}, u32[]{:S(2)}) copy-start(s32[128]{0:T(128)} %param.13) | copy-start | bytes 1540
  457.8 23.9 %all-to-all-start.3 = ((bf16[4,96,2048]{2,1,0:T(8,128)(2,1)}), bf16[4,96,2048]{2,1,0:T(8,128)(2,1)S(1)}, u32[]{:S(2)}, u32[]{:S(2)}) async-start(bf16[4,96,2048]{2,1,0:T(8,128)(2,1)} %bitcast.12), calls=%async_computation.3 | async-start | bytes 3145728 | tf_op jit(solution)/shard_map/all_to_all | solution.py:104
  461.4 129.0 %all-reduce.4.cloned.1.call-start = ((), (), s32[]{:S(2)}) async-start(), calls=%async_computation.6 | async-start | bytes 131072 | tf_op jit(solution)/shard_map/psum | solution.py:122
  481.7 1.2 copy-start.4
  493.3 1.4 copy-start.2
  496.1 179.9 %all-reduce.6.cloned.1.call-start = ((), (), s32[]{:S(2)}) async-start(), calls=%async_computation.7 | async-start | bytes 229376 | tf_op jit(solution)/shard_map/psum | solution.py:123
Sparse Core Ops, SparseCore 0:
  10.1 258.8 all-gather.2
  271.2 127.7 all-gather.4
  496.2 94.0 all-reduce.3
  594.0 81.9 all-reduce.5
